TPU v7x, 32 devices: a whole 2x2x4 slice. The times are simulated.
32 devices in a mesh: groups: 2 (over y), expert: 4 (over z), dp: 2 (over x), tile: 2 (over core).
Axes of the slice: x: 2, y: 2, z: 4, core: 2. Of those that a mesh axis runs over, the one named last changes fastest.
Arguments:
- features: bfloat16 [256, 1024], P(('groups', 'expert', 'dp', 'tile')), parts along dimension 0, may hold values from -6 to 6
- cross_weight: bfloat16 [1024, 1024], P(None, ('dp', 'tile')), may hold values from -0.1875 to 0.1875
- cross_bias: float32 [1024], replicated, may hold values from -1 to 1
- gate_weight: bfloat16 [1024, 36], replicated, may hold values from -24 to 24
- unit_experts: int32 [6, 6], replicated, may hold values from 0 to 15, all different within a row
- up_weight: bfloat16 [1024, 65536], P(None, ('expert', 'dp')), may hold values from -0.1875 to 0.1875
- up_bias: float32 [65536], P(('expert', 'dp')), may hold values from -3 to 3
- down_weight: bfloat16 [65536, 512], P(('expert', 'dp')), may hold values from -0.09375 to 0.09375
- down_bias: float32 [16, 512], replicated, may hold values from -3 to 3
- task_counts: int32 [32, 6], P(('groups', 'expert', 'dp', 'tile')), parts along dimension 0, may hold values from 1 to 8, as said below
- tower_in: bfloat16 [6, 512, 2048], P(None, None, ('dp', 'tile')), may hold values from -0.25 to 0.25
- tower_in_bias: float32 [6, 2048], P(None, ('dp', 'tile')), may hold values from -3 to 3
- tower_out: bfloat16 [6, 2048, 512], P(None, ('dp', 'tile')), may hold values from -0.125 to 0.125
- tower_out_bias: float32 [6, 512], replicated, may hold values from -3 to 3
Outputs:
- task_states: bfloat16 [256, 6, 512], P(('groups', 'expert', 'dp', 'tile')), parts along dimension 0
There are 2 independent parts, one for each index of `groups`. A program takes and returns all parts, laid end to end along the dimension named above; an argument that names none is the same for every part. Nothing has to cross between parts.
Inputs may be any that keep to these rules, and one draw needn't show every extreme that they name: `task_counts`: every task reaches a count of 8 on some row shard; which one is drawn from the seed.
All inputs are finite; a program needn't handle non-finite values.
Results may differ from a plain program's by a relative error of at most 0.0095.
Values may be sent and summed in bfloat16 or wider, within the bound.
A program may use at most 64 MiB of HBM per device.

v0:
```python
import jax
import jax.numpy as jnp
from jax import lax
from jax.sharding import PartitionSpec as P

EXPERT_FF = 4096


def body(
    features,
    cross_weight,
    cross_bias,
    gate_weight,
    unit_experts,
    up_weight,
    up_bias,
    down_weight,
    down_bias,
    task_counts,
    tower_in,
    tower_in_bias,
    tower_out,
    tower_out_bias,
):
    rows_own = features.shape[0]
    task_count = unit_experts.shape[0]
    unit_width = unit_experts.shape[1]
    out_width = down_weight.shape[1]
    column_base = features.astype(jnp.float32)
    scaled = (
        jnp.dot(
            features,
            lax.all_gather(cross_weight, ("dp", "tile"), axis=1, tiled=True),
            preferred_element_type=jnp.float32,
        )
        + cross_bias
    )
    crossed = (column_base * scaled + column_base).astype(jnp.bfloat16)
    logits = jnp.dot(features, gate_weight, preferred_element_type=jnp.float32)
    gate_probs = jax.nn.softmax(logits.reshape(rows_own, task_count, unit_width), axis=-1)
    hid_dev = up_weight.shape[1]
    pieces = max(1, hid_dev // EXPERT_FF)
    piece_width = hid_dev // pieces
    down_split = down_weight.reshape(pieces, piece_width, out_width)
    row_piece = lax.all_gather(crossed, ("expert", "dp"), axis=0, tiled=True)
    hidden = jnp.dot(row_piece, up_weight, preferred_element_type=jnp.float32) + up_bias
    hidden = (
        jax.nn.relu(hidden).astype(jnp.bfloat16).reshape(row_piece.shape[0], pieces, piece_width)
    )
    partial_value = jnp.einsum(
        "rpw,pwo->rpo", hidden, down_split, preferred_element_type=jnp.float32
    )
    expert_size = lax.axis_size("expert")
    data_size = lax.axis_size("dp")
    sources = expert_size * data_size
    blocks = partial_value.reshape(sources, rows_own, pieces, out_width)
    returned = lax.all_to_all(blocks, ("expert", "dp"), split_axis=0, concat_axis=0, tiled=True)
    per_expert = EXPERT_FF // piece_width
    ordered = jnp.moveaxis(returned, 2, 1).reshape(
        sources * pieces // per_expert, per_expert, rows_own, out_width
    )
    expert_out = jnp.sum(ordered, axis=1) + down_bias[:, None, :]
    onehot = (
        unit_experts[:, :, None] == jnp.arange(expert_out.shape[0], dtype=jnp.int32)[None, None, :]
    ).astype(jnp.float32)
    mix_weights = jnp.einsum("rtk,tke->rte", gate_probs, onehot)
    mixed_rows = jnp.einsum("rte,ero->rto", mix_weights, expert_out).astype(jnp.bfloat16)
    everyone = lax.all_gather(mixed_rows, ("dp", "tile"), axis=0, tiled=True)
    hidden = jnp.einsum("rto,toh->rth", everyone, tower_in, preferred_element_type=jnp.float32)
    hidden = jax.nn.relu(hidden + tower_in_bias[None, :, :]).astype(jnp.bfloat16)
    summed = lax.psum_scatter(
        jnp.einsum("rth,tho->rto", hidden, tower_out, preferred_element_type=jnp.float32),
        ("dp", "tile"),
        scatter_dimension=0,
        tiled=True,
    )
    tower_result = summed + tower_out_bias[None, :, :]
    position = jnp.arange(rows_own, dtype=jnp.int32)[:, None]
    active = position < task_counts
    return jnp.where(active[:, :, None], tower_result, 0.0).astype(jnp.bfloat16)


def solution(mesh):
    return jax.shard_map(
        body,
        mesh=mesh,
        in_specs=(
            P(("groups", "expert", "dp", "tile"), None),
            P(None, ("dp", "tile")),
            P(),
            P(),
            P(),
            P(None, ("expert", "dp")),
            P(("expert", "dp")),
            P(("expert", "dp"), None),
            P(),
            P(("groups", "expert", "dp", "tile"), None),
            P(None, None, ("dp", "tile")),
            P(None, ("dp", "tile")),
            P(None, ("dp", "tile"), None),
            P(),
        ),
        out_specs=P(("groups", "expert", "dp", "tile"), None, None),
        check_vma=False,
    )
```

profile of v0, /device:TPU:0, one launch (start us, length us, event | category | flops | bytes accessed | tf_op | source)
XLA Modules:
  0.0 128.5 jit_solution(7548105126115898000)
XLA Ops:
  6.5 0.0 copy-start
  6.5 0.0 all-gather.2.cloned.1.call-start
  6.5 0.7 all-gather.2.cloned.1.call-update
  7.3 1.3 fusion.21
  8.5 0.1 reshape.43
  8.6 25.9 %all-gather.2.cloned.1.call-done = bf16[1024,1024]{1,0:T(8,128)(2,1)} async-done(((bf16[1024,256]{1,0:T(8,128)(2,1)}), bf16[1024,1024]{1,0:T(8,128)(2,1)}) %all-gather.2.cloned.1.call-update) | async-done | bytes 2097168 | tf_op jit(solution)/shard_map/all_gather | solution.py:33
  34.5 0.0 slice-start
  34.5 2.1 %fusion.10 = bf16[8,1024]{1,0:T(8,128)(2,1)S(1)} fusion(bf16[8,1024]{1,0:T(8,128)(2,1)} %param.14, bf16[1024,1024]{1,0:T(8,128)(2,1)} %all-gather.2.cloned.1.call-done, f32[1024]{0:T(1024)} %param.16), kind=kOutput, calls=%fused_computation.16 | convolution fusion | flops 16818176 | bytes 2134016 | tf_op jit(solution)/shard_map/dot_general | solution.py:31
  36.6 30.6 %all_gather.10 = bf16[64,1024]{1,0:T(8,128)(2,1)S(1)} all-gather(bf16[8,1024]{1,0:T(8,128)(2,1)S(1)} %fusion.10), channel_id=1, replica_groups=mesh['groups'=2,'expert'=4,'dp'=2,'tile'=2] {'expert','dp'}, dimensions={0}, use_global_device_ids=true | all-gather | bytes 147456 | tf_op jit(solution)/shard_map/all_gather | solution.py:45
  67.2 0.0 slice-start.1
  67.2 8.9 %fusion.2 = bf16[64,8192]{1,0:T(8,128)(2,1)S(1)} fusion(bf16[64,1024]{1,0:T(8,128)(2,1)S(1)} %all_gather.10, bf16[1024,8192]{1,0:T(8,128)(2,1)} %param.19, f32[8192]{0:T(1024)} %param.20), kind=kOutput, calls=%fused_computation.3 | convolution fusion | flops 1075314688 | bytes 17989632 | tf_op jit(solution)/shard_map/dot_general | solution.py:46
  76.1 0.0 slice-done
  76.1 0.0 slice-done.1
  76.1 0.0 copy-start.4
  76.2 0.0 copy-start.1
  76.2 0.0 copy-start.2
  76.2 1.6 %convolution_bitcast_fusion.1 = f32[8,8,2,512]{3,1,0,2:T(8,128)S(1)} fusion(bf16[2,4096,512]{2,1,0:T(8,128)(2,1)S(1)} %bitcast.35, bf16[8,2,8,4096]{3,2,1,0:T(8,128)(2,1)S(1)} %bitcast.36), kind=kOutput, calls=%fused_computation.8 | convolution fusion | flops 536870912 | bytes 9699328 | tf_op jit(solution)/shard_map/rpw,pwo->rpo/dot_general | solution.py:50
  77.7 0.7 copy.20
  78.5 4.5 %all-to-all-start = ((f32[8,8,2,512]{3,1,2,0:T(8,128)}), f32[8,8,2,512]{3,1,2,0:T(8,128)S(1)}, u32[]{:S(2)}, u32[]{:S(2)}) async-start(f32[8,8,2,512]{3,1,2,0:T(8,128)} %copy.20), calls=%async_computation | async-start | bytes 524288 | tf_op jit(solution)/shard_map/all_to_all | solution.py:57
  83.0 0.0 reduce-scatter.2.cloned.1.call-start
  83.1 1.3 %fusion.20 = (f32[8,6]{1,0:T(8,128)S(1)}, f32[8,6,6]{2,1,0:T(8,128)S(1)}) fusion(f32[8,6,6]{2,1,0:T(8,128)S(1)} %reshape.43), kind=kOutput, calls=%fused_computation.32 | output fusion | flops 581 | bytes 2496 | tf_op jit(solution)/shard_map/sub | solution.py:40
  84.4 0.1 broadcast_divide_fusion
  84.5 0.0 copy-done.4
  84.5 0.2 convolution_bitcast_fusion.2
  84.7 6.5 %all-to-all-done = f32[8,8,2,512]{3,1,2,0:T(8,128)S(1)} async-done(((f32[8,8,2,512]{3,1,2,0:T(8,128)}), f32[8,8,2,512]{3,1,2,0:T(8,128)S(1)}, u32[]{:S(2)}, u32[]{:S(2)}) %all-to-all-start) | async-done | bytes 262176 | tf_op jit(solution)/shard_map/all_to_all | solution.py:57
  91.2 0.0 copy-done.1
  91.3 0.2 convolution_convert_fusion
  91.5 5.6 %all_gather.11 = bf16[32,6,512]{2,0,1:T(8,128)(2,1)S(1)} all-gather(bf16[8,6,512]{2,0,1:T(8,128)(2,1)S(1)} %copy.23), channel_id=1, replica_groups=mesh['groups'=2,'expert'=4,'dp'=2,'tile'=2] {'dp','tile'}, dimensions={0}, use_global_device_ids=true | all-gather | bytes 245760 | tf_op jit(solution)/shard_map/all_gather | solution.py:68
  97.1 0.0 copy-done
  97.1 0.0 copy-done.2
  97.1 0.0 copy-start.5
  97.1 0.0 copy-start.3
  97.1 3.8 %convolution_bitcast_fusion = f32[32,6,512]{2,0,1:T(8,128)} fusion(bf16[6,512,512]{2,1,0:T(8,128)(2,1)S(1)} %copy-done, bf16[32,6,512]{2,0,1:T(8,128)(2,1)S(1)} %all_gather.11, bf16[6,512,512]{2,1,0:T(8,128)(2,1)} %param.24, f32[6,512]{1,0:T(8,128)S(1)} %copy-done.2), kind=kOutput, calls=%fused_computation.4 | convolution fusion | flops 201621504 | bytes 6893568 | tf_op jit(solution)/shard_map/rth,tho->rto/dot_general | solution.py:72
  100.8 0.0 reduce-scatter.2.cloned.1.call-update
  100.9 0.0 copy-done.5
  100.9 0.1 iota_compare_fusion.2
  101.0 19.2 %reduce-scatter.2.cloned.1.call-done = f32[8,6,512]{2,0,1:T(8,128)} async-done(((f32[32,6,512]{2,0,1:T(8,128)}), f32[8,6,512]{2,0,1:T(8,128)}) %reduce-scatter.2.cloned.1.call-update) | async-done | bytes 98320 | tf_op jit(solution)/shard_map/reduce_scatter | solution.py:71
  120.1 0.0 copy-done.3
  120.1 1.6 %select_convert_fusion = bf16[8,6,512]{2,0,1:T(8,128)(2,1)} fusion(f32[8,6,512]{2,0,1:T(8,128)} %reduce-scatter.2.cloned.1.call-done, f32[6,512]{1,0:T(8,128)S(1)} %copy-done.3, pred[8,6]{0,1:T(8,128)(4,1)S(1)} %iota_compare_fusion.2), kind=kLoop, calls=%fused_computation.24 | loop fusion | flops 73728 | bytes 159792 | tf_op jit(solution)/shard_map/convert_element_type | solution.py:80
  (3 shorter events, 0.1 us)
Async XLA Ops:
  6.5 90.5 %copy-start = (bf16[6,512,512]{2,1,0:T(8,128)(2,1)S(1)}, bf16[6,512,512]{2,1,0:T(8,128)(2,1)}, u32[]{:S(2)}) copy-start(bf16[6,512,512]{2,1,0:T(8,128)(2,1)} %param.26) | copy-start | bytes 9437188
  6.5 27.9 %all-gather.2.cloned.1.call-start = ((), (), s32[]{:S(2)}) async-start(), calls=%async_computation.2 | async-start | bytes 2621440 | tf_op jit(solution)/shard_map/all_gather | solution.py:33
  34.5 41.7 %slice-start = ((s8[8388608]{0:T(1024)(128)(4,1)}), s8[4194304]{0:T(1024)(128)(4,1)S(1)}, s32[]{:S(2)}) async-start(s8[8388608]{0:T(1024)(128)(4,1)} %bitcast.33), calls=%async_computation.4 | async-start | bytes 8388608
  67.2 9.0 %slice-start.1 = ((s8[8388608]{0:T(1024)(128)(4,1)}), s8[4194304]{0:T(1024)(128)(4,1)S(1)}, s32[]{:S(2)}) async-start(s8[8388608]{0:T(1024)(128)(4,1)} %bitcast.33), calls=%async_computation.5 | async-start | bytes 8388608
  76.1 8.3 %copy-start.4 = (s32[6,6]{1,0:T(8,128)S(1)}, s32[6,6]{1,0:T(8,128)}, u32[]{:S(2)}) copy-start(s32[6,6]{1,0:T(8,128)} %param.18) | copy-start | bytes 436
  76.2 15.1 %copy-start.1 = (f32[16,512]{1,0:T(8,128)S(1)}, f32[16,512]{1,0:T(8,128)}, u32[]{:S(2)}) copy-start(f32[16,512]{1,0:T(8,128)} %param.22) | copy-start | bytes 98308
  76.2 20.9 %copy-start.2 = (f32[6,512]{1,0:T(8,128)S(1)}, f32[6,512]{1,0:T(8,128)}, u32[]{:S(2)}) copy-start(f32[6,512]{1,0:T(8,128)} %param.25) | copy-start | bytes 36868
  78.5 12.8 %all-to-all-start = ((f32[8,8,2,512]{3,1,2,0:T(8,128)}), f32[8,8,2,512]{3,1,2,0:T(8,128)S(1)}, u32[]{:S(2)}, u32[]{:S(2)}) async-start(f32[8,8,2,512]{3,1,2,0:T(8,128)} %copy.20), calls=%async_computation | async-start | bytes 524288 | tf_op jit(solution)/shard_map/all_to_all | solution.py:57
  83.0 37.1 %reduce-scatter.2.cloned.1.call-start = ((), (), s32[]{:S(2)}) async-start(), calls=%async_computation.3 | async-start | bytes 491520 | tf_op jit(solution)/shard_map/reduce_scatter | solution.py:71
  97.1 3.8 %copy-start.5 = (s32[1,6]{1,0:T(1,128)S(1)}, s32[1,6]{1,0:T(1,128)}, u32[]{:S(2)}) copy-start(s32[1,6]{1,0:T(1,128)} %param.23) | copy-start | bytes 76
  97.1 23.0 %copy-start.3 = (f32[6,512]{1,0:T(8,128)S(1)}, f32[6,512]{1,0:T(8,128)}, u32[]{:S(2)}) copy-start(f32[6,512]{1,0:T(8,128)} %param.27) | copy-start | bytes 36868
Sparse Core Ops, SparseCore 0:
  8.9 25.5 all-gather.1
  101.0 19.0 reduce-scatter.1
where the time goes:
time: 129 us
  waiting for transfers between devices  52.3 us (41%)
  blocking collectives  36.2 us (28%)
  matrix products  18 us (14%)
  between operations  13.5 us (10%)
  starting transfers between devices  4.57 us (4%)
  other arithmetic  3.11 us (2%)
    all_gather x1, blocking collectives, body(): row_piece = lax.all_gather(crossed, ('expert', 'dp'), axis=0, tiled=True)  30.6 us
    all_gather x1, waiting for transfers between devices, body(): lax.all_gather(cross_weight, ('dp', 'tile'), axis=1, tiled=True)  25.9 us
    reduce_scatter x1, waiting for transfers between devices, body(): lax.psum_scatter(jnp.einsum('rth,tho->rto', hidden, tower_out, preferred_...  19.2 us
    dot_general x1, matrix products, body(): jnp.dot(row_piece, up_weight, preferred_element_type=jnp.float32) + up_bias  8.94 us
    all_to_all x1, waiting for transfers between devices, body(): lax.all_to_all(blocks, ('expert', 'dp'), split_axis=0, concat_axis=0, til...  6.55 us
    all_gather x1, blocking collectives, body(): everyone = lax.all_gather(mixed_rows, ('dp', 'tile'), axis=0, tiled=True)  5.6 us
    all_to_all x1, starting transfers between devices, body(): lax.all_to_all(blocks, ('expert', 'dp'), split_axis=0, concat_axis=0, til...  4.53 us
    dot_general x1, matrix products, body(): jnp.einsum('rth,tho->rto', hidden, tower_out, preferred_element_type=jnp....  3.77 us
  transfers between devices with their start and end apart: 3, of which 3 were waited for; matrix products, arithmetic and copies ran while one was open for 2% of the time, Pallas kernels for 0%

commit v1 on v0

--- a/solution.py
+++ b/solution.py
@@ -42,7 +42,16 @@
     pieces = max(1, hid_dev // EXPERT_FF)
     piece_width = hid_dev // pieces
     down_split = down_weight.reshape(pieces, piece_width, out_width)
-    row_piece = lax.all_gather(crossed, ("expert", "dp"), axis=0, tiled=True)
+    ways = lax.axis_size(("expert", "dp"))
+    pieces_2 = [crossed]
+    for far in range(1, ways):
+        pieces_2.append(
+            lax.ppermute(
+                pieces_2[far - 1], ("expert", "dp"), [(d, (d - 1) % ways) for d in range(ways)]
+            )
+        )
+    line = jnp.concatenate(pieces_2, axis=0)
+    row_piece = jnp.roll(line, lax.axis_index(("expert", "dp")) * crossed.shape[0], axis=0)
     hidden = jnp.dot(row_piece, up_weight, preferred_element_type=jnp.float32) + up_bias
     hidden = (
         jax.nn.relu(hidden).astype(jnp.bfloat16).reshape(row_piece.shape[0], pieces, piece_width)

time: 129 us -> 144 us (1.12)
  starting transfers between devices: 4.57 us -> 39.7 us
  blocking collectives: 36.2 us -> 5.6 us
  waiting for transfers between devices: 52.3 us -> 62.6 us
    ppermute x0 -> x7, starting transfers between devices: none -> 33.4 us  [body(): lax.ppermute(pieces_2[far - 1], ('expert', 'dp'), [(d, (d - 1) % ways) fo...]
    all_gather x1 -> x0, blocking collectives: 30.6 us -> none  [body(): row_piece = lax.all_gather(crossed, ('expert', 'dp'), axis=0, tiled=True)]
    ppermute x0 -> x7, waiting for transfers between devices: none -> 8.98 us  [body(): lax.ppermute(pieces_2[far - 1], ('expert', 'dp'), [(d, (d - 1) % ways) fo...]
    all_to_all x1, starting transfers between devices: 4.53 us -> 6.27 us  [body(): lax.all_to_all(blocks, ('expert', 'dp'), split_axis=0, concat_axis=0, til...]
  transfers between devices with their start and end apart: 3 -> 10, of which waited for: 3 -> 10; matrix products, arithmetic and copies ran while one was open for 2% -> 2% of each run, Pallas kernels for 0% -> 0%
where the time goes in v1:
time: 144 us; the launch traced here: 143 us
  waiting for transfers between devices  62.6 us (43%)
  starting transfers between devices  39.7 us (28%)
  matrix products  17.6 us (12%)
  between operations  13.6 us (9%)
  blocking collectives  5.6 us (4%)
  other arithmetic  3.11 us (2%)
    ppermute x7, starting transfers between devices, body(): lax.ppermute(pieces_2[far - 1], ('expert', 'dp'), [(d, (d - 1) % ways) fo...  33.4 us
    all_gather x1, waiting for transfers between devices, body(): lax.all_gather(cross_weight, ('dp', 'tile'), axis=1, tiled=True)  27.2 us
    reduce_scatter x1, waiting for transfers between devices, body(): lax.psum_scatter(jnp.einsum('rth,tho->rto', hidden, tower_out, preferred_...  19.2 us
    ppermute x7, waiting for transfers between devices, body(): lax.ppermute(pieces_2[far - 1], ('expert', 'dp'), [(d, (d - 1) % ways) fo...  8.98 us
    dot_general x1, matrix products, body(): jnp.dot(row_piece, up_weight, preferred_element_type=jnp.float32) + up_bias  8.95 us
    all_to_all x1, waiting for transfers between devices, body(): lax.all_to_all(blocks, ('expert', 'dp'), split_axis=0, concat_axis=0, til...  6.55 us
    all_to_all x1, starting transfers between devices, body(): lax.all_to_all(blocks, ('expert', 'dp'), split_axis=0, concat_axis=0, til...  6.27 us
    all_gather x1, blocking collectives, body(): everyone = lax.all_gather(mixed_rows, ('dp', 'tile'), axis=0, tiled=True)  5.6 us
  transfers between devices with their start and end apart: 10, of which 10 were waited for; matrix products, arithmetic and copies ran while one was open for 2% of the time, Pallas kernels for 0%

profile of v1, /device:TPU:0, one launch (start us, length us, event | category | flops | bytes accessed | tf_op | source)
XLA Modules:
  0.0 143.2 jit_solution(8521217423959845287)
XLA Ops:
  6.5 0.0 copy-start
  6.5 0.0 all-gather.2.cloned.1.call-start
  6.5 0.7 all-gather.2.cloned.1.call-update
  7.3 27.2 %all-gather.2.cloned.1.call-done = bf16[1024,1024]{1,0:T(8,128)(2,1)} async-done(((bf16[1024,256]{1,0:T(8,128)(2,1)}), bf16[1024,1024]{1,0:T(8,128)(2,1)}) %all-gather.2.cloned.1.call-update) | async-done | bytes 2097168 | tf_op jit(solution)/shard_map/all_gather | solution.py:33
  34.5 2.0 %constant_dynamic-update-slice_fusion.15 = (bf16[128,1024]{1,0:T(8,128)(2,1)S(1)}, bf16[8,1024]{1,0:T(8,128)(2,1)S(1)}) fusion(f32[1024]{0:T(1024)} %param.16, bf16[8,1024]{1,0:T(8,128)(2,1)} %param.14, bf16[1024,1024]{1,0:T(8,128)(2,1)} %all-gather.2.cloned.1.call-done), kind=kOutput, calls=%fused_computation.41 | convolution fusion | flops 16818176 | bytes 2166784 | tf_op jit(solution)/shard_map/dot_general | solution.py:31
  36.4 3.3 %collective-permute-start = (bf16[8,1024]{1,0:T(8,128)(2,1)S(1)}, bf16[8,1024]{1,0:T(8,128)(2,1)S(1)}, u32[]{:S(2)}, u32[]{:S(2)}) collective-permute-start(bf16[8,1024]{1,0:T(8,128)(2,1)S(1)} %get-tuple-element.6), channel_id=1, source_target_pairs={{0,14},{2,0},{4,2},{6,4},{8,6},{10,8},{12,10},{14,12},{1,15},{3,1}... | collective-permute-start | bytes 49160 | tf_op jit(solution)/shard_map/ppermute | solution.py:49
  39.8 1.0 fusion.23
  40.8 0.1 reshape.43
  40.9 0.3 collective-permute-done
  41.2 5.0 %collective-permute-start.1 = (bf16[8,1024]{1,0:T(8,128)(2,1)S(1)}, bf16[8,1024]{1,0:T(8,128)(2,1)S(1)}, u32[]{:S(2)}, u32[]{:S(2)}) collective-permute-start(bf16[8,1024]{1,0:T(8,128)(2,1)S(1)} %collective-permute-done), channel_id=1, source_target_pairs={{0,14},{2,0},{4,2},{6,4},{8,6},{10,8},{12,10},{14,12},{1,15},{3,1}... | collective-permute-start | bytes 49160 | tf_op jit(solution)/shard_map/ppermute | solution.py:49
  46.2 1.4 %collective-permute-done.1 = bf16[8,1024]{1,0:T(8,128)(2,1)S(1)} collective-permute-done((bf16[8,1024]{1,0:T(8,128)(2,1)S(1)}, bf16[8,1024]{1,0:T(8,128)(2,1)S(1)}, u32[]{:S(2)}, u32[]{:S(2)}) %collective-permute-start.1) | collective-permute-done | bytes 16416 | tf_op jit(solution)/shard_map/ppermute | solution.py:49
  47.6 5.0 %collective-permute-start.2 = (bf16[8,1024]{1,0:T(8,128)(2,1)S(1)}, bf16[8,1024]{1,0:T(8,128)(2,1)S(1)}, u32[]{:S(2)}, u32[]{:S(2)}) collective-permute-start(bf16[8,1024]{1,0:T(8,128)(2,1)S(1)} %collective-permute-done.1), channel_id=1, source_target_pairs={{0,14},{2,0},{4,2},{6,4},{8,6},{10,8},{12,10},{14,12},{1,15},{3,1}... | collective-permute-start | bytes 49160 | tf_op jit(solution)/shard_map/ppermute | solution.py:49
  52.6 1.4 %collective-permute-done.2 = bf16[8,1024]{1,0:T(8,128)(2,1)S(1)} collective-permute-done((bf16[8,1024]{1,0:T(8,128)(2,1)S(1)}, bf16[8,1024]{1,0:T(8,128)(2,1)S(1)}, u32[]{:S(2)}, u32[]{:S(2)}) %collective-permute-start.2) | collective-permute-done | bytes 16416 | tf_op jit(solution)/shard_map/ppermute | solution.py:49
  54.1 5.0 %collective-permute-start.3 = (bf16[8,1024]{1,0:T(8,128)(2,1)S(1)}, bf16[8,1024]{1,0:T(8,128)(2,1)S(1)}, u32[]{:S(2)}, u32[]{:S(2)}) collective-permute-start(bf16[8,1024]{1,0:T(8,128)(2,1)S(1)} %collective-permute-done.2), channel_id=1, source_target_pairs={{0,14},{2,0},{4,2},{6,4},{8,6},{10,8},{12,10},{14,12},{1,15},{3,1}... | collective-permute-start | bytes 49160 | tf_op jit(solution)/shard_map/ppermute | solution.py:49
  59.1 1.4 %collective-permute-done.3 = bf16[8,1024]{1,0:T(8,128)(2,1)S(1)} collective-permute-done((bf16[8,1024]{1,0:T(8,128)(2,1)S(1)}, bf16[8,1024]{1,0:T(8,128)(2,1)S(1)}, u32[]{:S(2)}, u32[]{:S(2)}) %collective-permute-start.3) | collective-permute-done | bytes 16416 | tf_op jit(solution)/shard_map/ppermute | solution.py:49
  60.5 5.0 %collective-permute-start.4 = (bf16[8,1024]{1,0:T(8,128)(2,1)S(1)}, bf16[8,1024]{1,0:T(8,128)(2,1)S(1)}, u32[]{:S(2)}, u32[]{:S(2)}) collective-permute-start(bf16[8,1024]{1,0:T(8,128)(2,1)S(1)} %collective-permute-done.3), channel_id=1, source_target_pairs={{0,14},{2,0},{4,2},{6,4},{8,6},{10,8},{12,10},{14,12},{1,15},{3,1}... | collective-permute-start | bytes 49160 | tf_op jit(solution)/shard_map/ppermute | solution.py:49
  65.5 1.4 %collective-permute-done.4 = bf16[8,1024]{1,0:T(8,128)(2,1)S(1)} collective-permute-done((bf16[8,1024]{1,0:T(8,128)(2,1)S(1)}, bf16[8,1024]{1,0:T(8,128)(2,1)S(1)}, u32[]{:S(2)}, u32[]{:S(2)}) %collective-permute-start.4) | collective-permute-done | bytes 16416 | tf_op jit(solution)/shard_map/ppermute | solution.py:49
  67.0 5.1 %collective-permute-start.5 = (bf16[8,1024]{1,0:T(8,128)(2,1)S(1)}, bf16[8,1024]{1,0:T(8,128)(2,1)S(1)}, u32[]{:S(2)}, u32[]{:S(2)}) collective-permute-start(bf16[8,1024]{1,0:T(8,128)(2,1)S(1)} %collective-permute-done.4), channel_id=1, source_target_pairs={{0,14},{2,0},{4,2},{6,4},{8,6},{10,8},{12,10},{14,12},{1,15},{3,1}... | collective-permute-start | bytes 49160 | tf_op jit(solution)/shard_map/ppermute | solution.py:49
  72.1 1.4 %collective-permute-done.5 = bf16[8,1024]{1,0:T(8,128)(2,1)S(1)} collective-permute-done((bf16[8,1024]{1,0:T(8,128)(2,1)S(1)}, bf16[8,1024]{1,0:T(8,128)(2,1)S(1)}, u32[]{:S(2)}, u32[]{:S(2)}) %collective-permute-start.5) | collective-permute-done | bytes 16416 | tf_op jit(solution)/shard_map/ppermute | solution.py:49
  73.5 5.0 %collective-permute-start.6 = (bf16[8,1024]{1,0:T(8,128)(2,1)S(1)}, bf16[8,1024]{1,0:T(8,128)(2,1)S(1)}, u32[]{:S(2)}, u32[]{:S(2)}) collective-permute-start(bf16[8,1024]{1,0:T(8,128)(2,1)S(1)} %collective-permute-done.5), channel_id=1, source_target_pairs={{0,14},{2,0},{4,2},{6,4},{8,6},{10,8},{12,10},{14,12},{1,15},{3,1}... | collective-permute-start | bytes 49160 | tf_op jit(solution)/shard_map/ppermute | solution.py:49
  78.5 1.4 %collective-permute-done.6 = bf16[8,1024]{1,0:T(8,128)(2,1)S(1)} collective-permute-done((bf16[8,1024]{1,0:T(8,128)(2,1)S(1)}, bf16[8,1024]{1,0:T(8,128)(2,1)S(1)}, u32[]{:S(2)}, u32[]{:S(2)}) %collective-permute-start.6) | collective-permute-done | bytes 16416 | tf_op jit(solution)/shard_map/ppermute | solution.py:49
  80.1 0.0 copy-done.1
  80.1 0.0 slice-start.1
  80.1 8.9 %fusion.2 = bf16[64,8192]{1,0:T(8,128)(2,1)S(1)} fusion(bf16[1024,8192]{1,0:T(8,128)(2,1)} %param.19, f32[8192]{0:T(1024)S(1)} %copy-done.1, bf16[128,1024]{1,0:T(8,128)(2,1)S(1)} %constant_dynamic-update-slice_fusion, s32[]{:T(128)S(6)} %select_n.18), kind=kOutput, calls=%fused_computation.3 | convolution fusion | flops 1075314688 | bytes 17989636 | tf_op jit(solution)/shard_map/dot_general | solution.py:55
  89.0 0.0 slice-done
  89.0 0.0 slice-done.1
  89.1 0.0 copy-start.5
  89.1 0.0 copy-start.2
  89.1 0.0 copy-start.3
  89.1 1.6 %convolution_bitcast_fusion.1 = f32[8,8,2,512]{3,1,0,2:T(8,128)S(1)} fusion(bf16[2,4096,512]{2,1,0:T(8,128)(2,1)S(1)} %bitcast.34, bf16[8,2,8,4096]{3,2,1,0:T(8,128)(2,1)S(1)} %bitcast.35), kind=kOutput, calls=%fused_computation.8 | convolution fusion | flops 536870912 | bytes 9699328 | tf_op jit(solution)/shard_map/rpw,pwo->rpo/dot_general | solution.py:59
  90.7 0.7 copy.20
  91.4 6.3 %all-to-all-start = ((f32[8,8,2,512]{3,1,2,0:T(8,128)}), f32[8,8,2,512]{3,1,2,0:T(8,128)S(1)}, u32[]{:S(2)}, u32[]{:S(2)}) async-start(f32[8,8,2,512]{3,1,2,0:T(8,128)} %copy.20), calls=%async_computation | async-start | bytes 524288 | tf_op jit(solution)/shard_map/all_to_all | solution.py:66
  97.6 0.0 reduce-scatter.2.cloned.1.call-start
  97.7 1.3 fusion.22
  99.0 0.1 broadcast_divide_fusion
  99.1 0.0 copy-done.5
  99.1 0.2 convolution_bitcast_fusion.2
  99.3 6.5 %all-to-all-done = f32[8,8,2,512]{3,1,2,0:T(8,128)S(1)} async-done(((f32[8,8,2,512]{3,1,2,0:T(8,128)}), f32[8,8,2,512]{3,1,2,0:T(8,128)S(1)}, u32[]{:S(2)}, u32[]{:S(2)}) %all-to-all-start) | async-done | bytes 262176 | tf_op jit(solution)/shard_map/all_to_all | solution.py:66
  105.9 0.0 copy-done.2
  105.9 0.2 convolution_convert_fusion
  106.1 5.6 %all_gather.7 = bf16[32,6,512]{2,0,1:T(8,128)(2,1)S(1)} all-gather(bf16[8,6,512]{2,0,1:T(8,128)(2,1)S(1)} %copy.23), channel_id=1, replica_groups=mesh['groups'=2,'expert'=4,'dp'=2,'tile'=2] {'dp','tile'}, dimensions={0}, use_global_device_ids=true | all-gather | bytes 245760 | tf_op jit(solution)/shard_map/all_gather | solution.py:77
  111.7 0.0 copy-done
  111.7 3.8 %convolution_bitcast_fusion = f32[32,6,512]{2,0,1:T(8,128)} fusion(bf16[6,512,512]{2,1,0:T(8,128)(2,1)S(1)} %copy-done, bf16[32,6,512]{2,0,1:T(8,128)(2,1)S(1)} %all_gather.7, bf16[6,512,512]{2,1,0:T(8,128)(2,1)} %param.24, f32[6,512]{1,0:T(8,128)S(1)} %copy-done.3), kind=kOutput, calls=%fused_computation.4 | convolution fusion | flops 201621504 | bytes 6893568 | tf_op jit(solution)/shard_map/rth,tho->rto/dot_general | solution.py:81
  115.5 0.0 reduce-scatter.2.cloned.1.call-update
  115.5 0.1 iota_compare_fusion.2
  115.6 19.2 %reduce-scatter.2.cloned.1.call-done = f32[8,6,512]{2,0,1:T(8,128)} async-done(((f32[32,6,512]{2,0,1:T(8,128)}), f32[8,6,512]{2,0,1:T(8,128)}) %reduce-scatter.2.cloned.1.call-update) | async-done | bytes 98320 | tf_op jit(solution)/shard_map/reduce_scatter | solution.py:80
  134.7 0.0 copy-done.4
  134.7 1.6 %select_convert_fusion = bf16[8,6,512]{2,0,1:T(8,128)(2,1)} fusion(f32[8,6,512]{2,0,1:T(8,128)} %reduce-scatter.2.cloned.1.call-done, f32[6,512]{1,0:T(8,128)S(1)} %copy-done.4, pred[8,6]{0,1:T(8,128)(4,1)S(1)} %iota_compare_fusion.2), kind=kLoop, calls=%fused_computation.25 | loop fusion | flops 73728 | bytes 159792 | tf_op jit(solution)/shard_map/convert_element_type | solution.py:89
  (24 shorter events, 0.1 us)
Async XLA Ops:
  6.5 105.2 %copy-start = (bf16[6,512,512]{2,1,0:T(8,128)(2,1)S(1)}, bf16[6,512,512]{2,1,0:T(8,128)(2,1)}, u32[]{:S(2)}) copy-start(bf16[6,512,512]{2,1,0:T(8,128)(2,1)} %param.26) | copy-start | bytes 9437188
  6.5 73.5 %copy-start.1 = (f32[8192]{0:T(1024)S(1)}, f32[8192]{0:T(1024)}, u32[]{:S(2)}) copy-start(f32[8192]{0:T(1024)} %param.20) | copy-start | bytes 98308
  6.5 27.9 %all-gather.2.cloned.1.call-start = ((), (), s32[]{:S(2)}) async-start(), calls=%async_computation.2 | async-start | bytes 2621440 | tf_op jit(solution)/shard_map/all_gather | solution.py:33
  36.4 4.8 %collective-permute-start = (bf16[8,1024]{1,0:T(8,128)(2,1)S(1)}, bf16[8,1024]{1,0:T(8,128)(2,1)S(1)}, u32[]{:S(2)}, u32[]{:S(2)}) collective-permute-start(bf16[8,1024]{1,0:T(8,128)(2,1)S(1)} %get-tuple-element.6), channel_id=1, source_target_pairs={{0,14},{2,0},{4,2},{6,4},{8,6},{10,8},{12,10},{14,12},{1,15},{3,1}... | collective-permute-start | bytes 49160 | tf_op jit(solution)/shard_map/ppermute | solution.py:49
  41.2 6.4 %collective-permute-start.1 = (bf16[8,1024]{1,0:T(8,128)(2,1)S(1)}, bf16[8,1024]{1,0:T(8,128)(2,1)S(1)}, u32[]{:S(2)}, u32[]{:S(2)}) collective-permute-start(bf16[8,1024]{1,0:T(8,128)(2,1)S(1)} %collective-permute-done), channel_id=1, source_target_pairs={{0,14},{2,0},{4,2},{6,4},{8,6},{10,8},{12,10},{14,12},{1,15},{3,1}... | collective-permute-start | bytes 49160 | tf_op jit(solution)/shard_map/ppermute | solution.py:49
  47.6 6.4 %collective-permute-start.2 = (bf16[8,1024]{1,0:T(8,128)(2,1)S(1)}, bf16[8,1024]{1,0:T(8,128)(2,1)S(1)}, u32[]{:S(2)}, u32[]{:S(2)}) collective-permute-start(bf16[8,1024]{1,0:T(8,128)(2,1)S(1)} %collective-permute-done.1), channel_id=1, source_target_pairs={{0,14},{2,0},{4,2},{6,4},{8,6},{10,8},{12,10},{14,12},{1,15},{3,1}... | collective-permute-start | bytes 49160 | tf_op jit(solution)/shard_map/ppermute | solution.py:49
  54.1 6.4 %collective-permute-start.3 = (bf16[8,1024]{1,0:T(8,128)(2,1)S(1)}, bf16[8,1024]{1,0:T(8,128)(2,1)S(1)}, u32[]{:S(2)}, u32[]{:S(2)}) collective-permute-start(bf16[8,1024]{1,0:T(8,128)(2,1)S(1)} %collective-permute-done.2), channel_id=1, source_target_pairs={{0,14},{2,0},{4,2},{6,4},{8,6},{10,8},{12,10},{14,12},{1,15},{3,1}... | collective-permute-start | bytes 49160 | tf_op jit(solution)/shard_map/ppermute | solution.py:49
  60.5 6.4 %collective-permute-start.4 = (bf16[8,1024]{1,0:T(8,128)(2,1)S(1)}, bf16[8,1024]{1,0:T(8,128)(2,1)S(1)}, u32[]{:S(2)}, u32[]{:S(2)}) collective-permute-start(bf16[8,1024]{1,0:T(8,128)(2,1)S(1)} %collective-permute-done.3), channel_id=1, source_target_pairs={{0,14},{2,0},{4,2},{6,4},{8,6},{10,8},{12,10},{14,12},{1,15},{3,1}... | collective-permute-start | bytes 49160 | tf_op jit(solution)/shard_map/ppermute | solution.py:49
  67.0 6.6 %collective-permute-start.5 = (bf16[8,1024]{1,0:T(8,128)(2,1)S(1)}, bf16[8,1024]{1,0:T(8,128)(2,1)S(1)}, u32[]{:S(2)}, u32[]{:S(2)}) collective-permute-start(bf16[8,1024]{1,0:T(8,128)(2,1)S(1)} %collective-permute-done.4), channel_id=1, source_target_pairs={{0,14},{2,0},{4,2},{6,4},{8,6},{10,8},{12,10},{14,12},{1,15},{3,1}... | collective-permute-start | bytes 49160 | tf_op jit(solution)/shard_map/ppermute | solution.py:49
  73.5 6.4 %collective-permute-start.6 = (bf16[8,1024]{1,0:T(8,128)(2,1)S(1)}, bf16[8,1024]{1,0:T(8,128)(2,1)S(1)}, u32[]{:S(2)}, u32[]{:S(2)}) collective-permute-start(bf16[8,1024]{1,0:T(8,128)(2,1)S(1)} %collective-permute-done.5), channel_id=1, source_target_pairs={{0,14},{2,0},{4,2},{6,4},{8,6},{10,8},{12,10},{14,12},{1,15},{3,1}... | collective-permute-start | bytes 49160 | tf_op jit(solution)/shard_map/ppermute | solution.py:49
  80.0 9.1 %slice-start = ((s8[8388608]{0:T(1024)(128)(4,1)}), s8[4194304]{0:T(1024)(128)(4,1)S(1)}, s32[]{:S(2)}) async-start(s8[8388608]{0:T(1024)(128)(4,1)} %bitcast.32), calls=%async_computation.4 | async-start | bytes 8388608
  80.1 9.0 %slice-start.1 = ((s8[8388608]{0:T(1024)(128)(4,1)}), s8[4194304]{0:T(1024)(128)(4,1)S(1)}, s32[]{:S(2)}) async-start(s8[8388608]{0:T(1024)(128)(4,1)} %bitcast.32), calls=%async_computation.5 | async-start | bytes 8388608
  89.1 10.1 %copy-start.5 = (s32[6,6]{1,0:T(8,128)S(1)}, s32[6,6]{1,0:T(8,128)}, u32[]{:S(2)}) copy-start(s32[6,6]{1,0:T(8,128)} %param.18) | copy-start | bytes 436
  89.1 16.8 %copy-start.2 = (f32[16,512]{1,0:T(8,128)S(1)}, f32[16,512]{1,0:T(8,128)}, u32[]{:S(2)}) copy-start(f32[16,512]{1,0:T(8,128)} %param.22) | copy-start | bytes 98308
  89.1 22.6 %copy-start.3 = (f32[6,512]{1,0:T(8,128)S(1)}, f32[6,512]{1,0:T(8,128)}, u32[]{:S(2)}) copy-start(f32[6,512]{1,0:T(8,128)} %param.25) | copy-start | bytes 36868
  91.4 14.5 %all-to-all-start = ((f32[8,8,2,512]{3,1,2,0:T(8,128)}), f32[8,8,2,512]{3,1,2,0:T(8,128)S(1)}, u32[]{:S(2)}, u32[]{:S(2)}) async-start(f32[8,8,2,512]{3,1,2,0:T(8,128)} %copy.20), calls=%async_computation | async-start | bytes 524288 | tf_op jit(solution)/shard_map/all_to_all | solution.py:66
  97.6 37.1 %reduce-scatter.2.cloned.1.call-start = ((), (), s32[]{:S(2)}) async-start(), calls=%async_computation.3 | async-start | bytes 491520 | tf_op jit(solution)/shard_map/reduce_scatter | solution.py:80
  111.7 3.8 %copy-start.6 = (s32[1,6]{1,0:T(1,128)S(1)}, s32[1,6]{1,0:T(1,128)}, u32[]{:S(2)}) copy-start(s32[1,6]{1,0:T(1,128)} %param.23) | copy-start | bytes 76
  111.7 23.0 %copy-start.4 = (f32[6,512]{1,0:T(8,128)S(1)}, f32[6,512]{1,0:T(8,128)}, u32[]{:S(2)}) copy-start(f32[6,512]{1,0:T(8,128)} %param.27) | copy-start | bytes 36868
Sparse Core Ops, SparseCore 0:
  8.9 25.5 all-gather.1
  115.6 19.0 reduce-scatter.1
